TPU v7x, 32 devices: a whole 2x2x4 slice. The times are simulated.
32 devices in a mesh: tok: 8 (over z, core), rep: 4 (over y, x).
Axes of the slice: x: 2, y: 2, z: 4, core: 2. Of those that a mesh axis runs over, the one named last changes fastest.
Arguments:
- hidden_in: bfloat16 [4096, 4096], P('tok', 'rep'), may hold values from -9 to 9
- w_query: bfloat16 [4096, 4096], P(None, 'rep'), may hold values from -2 to 2
- w_key: bfloat16 [4096, 4096], P(None, 'rep'), may hold values from -2 to 2
- w_value: bfloat16 [4096, 4096], P(None, 'rep'), may hold values from -0.09375 to 0.09375
- w_out: bfloat16 [4096, 4096], P('rep'), may hold values from -3 to 3
- q_gain: float32 [4096], P('rep'), may hold values from 0.5 to 6
- k_gain: float32 [4096], P('rep'), may hold values from 0.5 to 6
- post_gain: float32 [4096], P('rep'), may hold values from 0.1 to 1.9
- prompt_lengths: int32 [8], replicated, may hold values from 1 to 2048, as said below
- segment_ids: int32 [4096], replicated, may hold values from 0 to 7, as said below
- deal: int32 [4096], replicated, may hold values from 0 to 4095, as said below
- inverse: int32 [4096], replicated, may hold values from 0 to 4095, as said below
- slots: int32 [4096], replicated, may hold values from 0 to 4095, as said below
Outputs:
- output: bfloat16 [4096, 4096], P('tok', 'rep')
- cache_keys: bfloat16 [4096, 4096], P('tok', 'rep')
- cache_values: bfloat16 [4096, 4096], P('tok', 'rep')
Inputs may be any that keep to these rules, and one draw needn't show every extreme that they name: `prompt_lengths`: the lengths sum to 4096; the longest prompt has exactly 2048 tokens. `segment_ids`: prompts lie in order: prompt s holds the prompt_lengths[s] packed tokens after those of prompts 0 to s - 1. `deal`: A permutation. For any two indices a and b of tok, exactly 64 of the packed tokens a * 512 to (a + 1) * 512 - 1 sit in dealt rows b * 512 to (b + 1) * 512 - 1. inverse[deal[q]] = q for every dealt row q. `slots`: A permutation. For any two indices a and b of tok, exactly 64 of the dealt rows a * 512 to (a + 1) * 512 - 1 have cache rows b * 512 to (b + 1) * 512 - 1.
All inputs are finite; a program needn't handle non-finite values.
Results may differ from a plain program's by a relative error of at most 0.012.
Values may be sent and summed in bfloat16 or wider, within the bound.
A program may use at most 128 MiB of HBM per device.

v0:
```python
import math
import jax
import jax.numpy as jnp
from jax import lax
from jax.sharding import PartitionSpec as P

HEAD_DIM = 128
EPSILON = 1e-06
ROPE_BASE = 500000.0


def rotate(values, positions):
    half_size = values.shape[-1] // 2
    frequency = ROPE_BASE ** (-jnp.arange(half_size, dtype=jnp.float32) * 2.0 / values.shape[-1])
    angles = positions.astype(jnp.float32)[:, None] * frequency[None, :]
    cosine = jnp.cos(angles)[:, None, :]
    sine_part = jnp.sin(angles)[:, None, :]
    lower_half = values[..., :half_size]
    upper_half = values[..., half_size:]
    return jnp.concatenate(
        [
            lower_half * cosine - upper_half * sine_part,
            upper_half * cosine + lower_half * sine_part,
        ],
        axis=-1,
    )


def bucketed(table_rows, row_order, shards):
    picked = table_rows[row_order]
    return picked.reshape(shards, picked.shape[0] // shards, picked.shape[1])


def placement_order(sources, shard_rows):
    local_ids = jnp.arange(sources.shape[0], dtype=jnp.int32)
    arrival = jnp.argsort(sources * shard_rows + local_ids)
    return jnp.argsort(arrival)


def body(
    hidden_in,
    w_query,
    w_key,
    w_value,
    w_out,
    q_gain,
    k_gain,
    post_gain,
    prompt_lengths,
    segment_ids,
    deal,
    inverse,
    slots,
):
    tok_rows, width_dev = hidden_in.shape
    full_width = w_query.shape[0]
    head_size = HEAD_DIM
    heads_dev = width_dev // head_size
    shards = lax.axis_size("tok")
    first_row = lax.axis_index("tok") * tok_rows
    my_packed = lax.dynamic_slice_in_dim(deal, first_row, tok_rows)
    my_segment = segment_ids[my_packed]
    prompt_ids = jnp.arange(prompt_lengths.shape[0], dtype=jnp.int32)
    prompt_starts = jnp.cumsum(prompt_lengths) - prompt_lengths
    my_start = jnp.sum(
        jnp.where(my_segment[:, None] == prompt_ids[None, :], prompt_starts[None, :], 0), axis=1
    )
    positions = my_packed - my_start
    pieces = lax.all_gather(hidden_in, "rep", axis=1, tiled=True)
    query_rows = jnp.dot(pieces, w_query, preferred_element_type=jnp.float32)
    key_rows = jnp.dot(pieces, w_key, preferred_element_type=jnp.float32)
    value_rows = jnp.dot(pieces, w_value, preferred_element_type=jnp.float32)
    query_sums, key_sums = lax.psum(
        (jnp.sum(query_rows * query_rows, axis=1), jnp.sum(key_rows * key_rows, axis=1)), "rep"
    )
    query_rows = (
        query_rows * lax.rsqrt(query_sums / full_width + EPSILON)[:, None] * q_gain[None, :]
    )
    key_rows = key_rows * lax.rsqrt(key_sums / full_width + EPSILON)[:, None] * k_gain[None, :]
    query_rot = rotate(query_rows.reshape(tok_rows, heads_dev, head_size), positions).astype(
        jnp.bfloat16
    )
    key_rot = (
        rotate(key_rows.reshape(tok_rows, heads_dev, head_size), positions)
        .astype(jnp.bfloat16)
        .reshape(tok_rows, width_dev)
    )
    value_half = value_rows.astype(jnp.bfloat16)
    scale = head_size ** (-0.5)

    def attend(state_now, key_block, value_block, key_packed):
        row_top, totals, weighted = state_now
        block_keys = key_block.reshape(key_block.shape[0], heads_dev, head_size)
        block_values = value_block.reshape(value_block.shape[0], heads_dev, head_size)
        key_segment = segment_ids[key_packed]
        allowed = (key_segment[None, :] == my_segment[:, None]) & (
            key_packed[None, :] <= my_packed[:, None]
        )
        scores = (
            jnp.einsum("qhd,khd->hqk", query_rot, block_keys, preferred_element_type=jnp.float32)
            * scale
        )
        masked = jnp.where(allowed[None], scores, -1e30)
        new_top = jnp.maximum(row_top, jnp.max(masked, axis=2))
        weights = jnp.where(allowed[None], jnp.exp(masked - new_top[:, :, None]), 0.0)
        factor = jnp.exp(row_top - new_top)
        totals = totals * factor + jnp.sum(weights, axis=2)
        weighted = weighted * factor[:, :, None] + jnp.einsum(
            "hqk,khd->hqd",
            weights.astype(jnp.bfloat16),
            block_values,
            preferred_element_type=jnp.float32,
        )
        return (new_top, totals, weighted)

    start_state = (
        jnp.full((heads_dev, tok_rows), -1e30, jnp.float32),
        jnp.zeros((heads_dev, tok_rows), jnp.float32),
        jnp.zeros((heads_dev, tok_rows, head_size), jnp.float32),
    )
    owned_rows = lax.dynamic_slice_in_dim(jnp.argsort(slots), first_row, tok_rows)
    my_slots = lax.dynamic_slice_in_dim(slots, first_row, tok_rows)
    slot_order = jnp.argsort(my_slots)
    sent_keys, sent_values = (
        lax.all_to_all(
            bucketed(key_rot, slot_order, shards), "tok", split_axis=0, concat_axis=0, tiled=True
        ),
        lax.all_to_all(
            bucketed(value_half, slot_order, shards), "tok", split_axis=0, concat_axis=0, tiled=True
        ),
    )
    arrival = placement_order(owned_rows // tok_rows, tok_rows)
    cache_keys = sent_keys.reshape(tok_rows, width_dev)[arrival]
    cache_values = sent_values.reshape(tok_rows, width_dev)[arrival]
    pieces = (
        lax.all_gather(key_rot, "tok", axis=0, tiled=True),
        lax.all_gather(value_half, "tok", axis=0, tiled=True),
    )
    key_all = pieces[0]
    block_size = math.gcd(key_all.shape[0], tok_rows)
    block_count = key_all.shape[0] // block_size

    def advance(state_in, block_set):
        return (attend(state_in, block_set[0], block_set[1], block_set[2]), None)

    state_out, _ = lax.scan(
        advance,
        start_state,
        (
            key_all.reshape(block_count, block_size, width_dev),
            pieces[1].reshape(block_count, block_size, width_dev),
            deal.reshape(block_count, block_size),
        ),
    )
    row_top, totals, weighted = state_out
    attended = (
        (weighted / totals[:, :, None])
        .transpose(1, 0, 2)
        .reshape(tok_rows, width_dev)
        .astype(jnp.bfloat16)
    )
    mixed_rows = (
        lax.psum_scatter(
            lax.dot_general(
                w_out, attended, (((0,), (1,)), ((), ())), preferred_element_type=jnp.float32
            ).astype(jnp.bfloat16),
            "rep",
            scatter_dimension=0,
            tiled=True,
        )
        .astype(jnp.float32)
        .T
    )
    mixed_sums = lax.psum(jnp.sum(mixed_rows * mixed_rows, axis=1), "rep")
    normed_rows = (
        mixed_rows * lax.rsqrt(mixed_sums / full_width + EPSILON)[:, None] * post_gain[None, :]
    )
    result_rows = (hidden_in.astype(jnp.float32) + normed_rows).astype(jnp.bfloat16)
    packed_order = jnp.argsort(my_packed)
    returned = lax.all_to_all(
        bucketed(result_rows, packed_order, shards), "tok", split_axis=0, concat_axis=0, tiled=True
    )
    my_dealt = lax.dynamic_slice_in_dim(inverse, first_row, tok_rows)
    output = returned.reshape(tok_rows, width_dev)[placement_order(my_dealt // tok_rows, tok_rows)]
    return (output, cache_keys, cache_values)


def solution(mesh):
    return jax.shard_map(
        body,
        mesh=mesh,
        in_specs=(
            P("tok", "rep"),
            P(None, "rep"),
            P(None, "rep"),
            P(None, "rep"),
            P("rep", None),
            P("rep"),
            P("rep"),
            P("rep"),
            P(),
            P(),
            P(),
            P(),
            P(),
        ),
        out_specs=(P("tok", "rep"), P("tok", "rep"), P("tok", "rep")),
        check_vma=False,
    )
```

profile of v0, /device:TPU:0, one launch (start us, length us, event | category | flops | bytes accessed | tf_op | source)
XLA Modules:
  0.0 586.3 jit_solution(2845161934136654388)
XLA Ops:
  13.8 51.3 %all-gather.4.cloned.1.call-done = bf16[512,4096]{1,0:T(8,128)(2,1)} async-done(((bf16[512,1024]{1,0:T(8,128)(2,1)}), bf16[512,4096]{1,0:T(8,128)(2,1)}) %all-gather.4.cloned.1.call-update) | async-done | bytes 4194320 | tf_op jit(solution)/shard_map/all_gather | solution.py:69
  65.2 10.6 %multiply_reduce_fusion.1 = (f32[512]{0:T(512)S(1)}, f32[512,1024]{1,0:T(8,128)}) fusion(bf16[512,4096]{1,0:T(8,128)(2,1)} %all-gather.4.cloned.1.call-done, bf16[4096,1024]{1,0:T(8,128)(2,1)} %param.17), kind=kOutput, calls=%fused_computation.47 | convolution fusion | flops 4296015360 | bytes 14682112 | tf_op jit(solution)/shard_map/dot_general | solution.py:71
  75.8 7.0 %multiply_reduce_fusion = (f32[512]{0:T(512)S(1)}, f32[512,1024]{1,0:T(8,128)S(1)}) fusion(bf16[512,4096]{1,0:T(8,128)(2,1)S(1)} %copy-done.8, bf16[4096,1024]{1,0:T(8,128)(2,1)} %param.16), kind=kOutput, calls=%fused_computation.43 | convolution fusion | flops 4296015360 | bytes 14682112 | tf_op jit(solution)/shard_map/dot_general | solution.py:70
  82.8 8.9 %all-reduce = (f32[512]{0:T(512)S(1)}, f32[512]{0:T(512)S(1)}) all-reduce(f32[512]{0:T(512)S(1)} %get-tuple-element.181, f32[512]{0:T(512)S(1)} %get-tuple-element.183), channel_id=1, replica_groups=mesh['tok'=8,'rep'=4] {'rep'}, use_global_device_ids=true, to_apply=%region_1.2 | all-reduce | flops 1024 | bytes 8192 | tf_op jit(solution)/shard_map/psum | solution.py:73
  99.6 10.1 %convolution_convert_fusion.1 = bf16[512,1024]{1,0:T(8,128)(2,1)} fusion(bf16[512,4096]{1,0:T(8,128)(2,1)} %all-gather.4.cloned.1.call-done, bf16[4096,1024]{1,0:T(8,128)(2,1)} %param.18), kind=kOutput, calls=%fused_computation.48 | convolution fusion | flops 4295491584 | bytes 13631488 | tf_op jit(solution)/shard_map/dot_general | solution.py:72
  111.4 70.1 %all-gather.6.cloned.1.call-done = bf16[4096,1024]{1,0:T(8,128)(2,1)} async-done(((bf16[512,1024]{1,0:T(8,128)(2,1)}), bf16[4096,1024]{1,0:T(8,128)(2,1)}) %all-gather.6.cloned.1.call-update) | async-done | bytes 8388624 | tf_op jit(solution)/shard_map/all_gather | solution.py:136
  181.6 82.7 %all-gather.8.cloned.1.call-done = bf16[4096,1024]{1,0:T(8,128)(2,1)} async-done(((bf16[512,1024]{1,0:T(8,128)(2,1)}), bf16[4096,1024]{1,0:T(8,128)(2,1)}) %all-gather.8.cloned.1.call-update) | async-done | bytes 8388624 | tf_op jit(solution)/shard_map/all_gather | solution.py:137
  264.3 202.6 %while.15 = (s32[]{:T(128)}, f32[8,512]{1,0:T(8,128)S(1)}, f32[8,512]{1,0:T(8,128)S(1)}, f32[8,512,128]{2,1,0:T(8,128)}, s32[8,512]{1,0:T(8,128)S(1)}, /*index=5...) while((s32[]{:T(128)}, f32[8,512]{1,0:T(8,128)S(1)}, ...), condition=%wide.region_9.10_spmd.clone, body=%wide.region_6.9_spmd.clone.sunk | while | flops 1103387136 | bytes 42231948 | solution.py:146
  270.0 6.1 %fusion.52 = (f32[8,512]{1,0:T(8,128)S(1)}, f32[8,512,512]{2,1,0:T(8,128)}) fusion(pred[512,512]{0,1:T(8,128)(4,1)S(1)} %compare_and_fusion.2, bf16[512,8,128]{0,2,1:T(8,128)(2,1)S(1)} %bitcast.85, bf16[512,8,128]{2,0,1:T(8,128)(2,1)} %get-tuple-element.307), kind=kOutput, calls=%fused_computation.10.clone.1 | convolution fusion | flops 543158272 | bytes 10764288 | tf_op jit(solution)/shard_map/while/body/eval_jaxpr/qhd,khd->hqk/dot_general | solution.py:100
  281.2 7.9 %fusion.55 = f32[8,512,128]{2,1,0:T(8,128)} fusion(f32[8,512,128]{2,1,0:T(8,128)} %get-tuple-element.288, bf16[512,8,128]{0,2,1:T(8,128)(2,1)S(1)} %bitcast.89, f32[8,512,512]{2,1,0:T(8,128)} %get-tuple-element.268, f32[8,512]{1,0:T(8,128)S(1)} %select_maximum_fusion.2, pred[512,512]{0,1:T(8,128)(4,1)S(1)} %compare_and_fusion.2, ...), kind=kOutput, calls=%fused_computation.16.clone.1 | convolution fusion | flops 548929536 | bytes 13926401 | tf_op jit(solution)/shard_map/while/body/eval_jaxpr/hqk,khd->hqd/dot_general | solution.py:108
  294.8 6.1 %fusion.52 = (f32[8,512]{1,0:T(8,128)S(1)}, f32[8,512,512]{2,1,0:T(8,128)}) fusion(pred[512,512]{0,1:T(8,128)(4,1)S(1)} %compare_and_fusion.2, bf16[512,8,128]{0,2,1:T(8,128)(2,1)S(1)} %bitcast.85, bf16[512,8,128]{2,0,1:T(8,128)(2,1)} %get-tuple-element.307), kind=kOutput, calls=%fused_computation.10.clone.1 | convolution fusion | flops 543158272 | bytes 10764288 | tf_op jit(solution)/shard_map/while/body/eval_jaxpr/qhd,khd->hqk/dot_general | solution.py:100
  306.0 8.5 %fusion.55 = f32[8,512,128]{2,1,0:T(8,128)} fusion(f32[8,512,128]{2,1,0:T(8,128)} %get-tuple-element.288, bf16[512,8,128]{0,2,1:T(8,128)(2,1)S(1)} %bitcast.89, f32[8,512,512]{2,1,0:T(8,128)} %get-tuple-element.268, f32[8,512]{1,0:T(8,128)S(1)} %select_maximum_fusion.2, pred[512,512]{0,1:T(8,128)(4,1)S(1)} %compare_and_fusion.2, ...), kind=kOutput, calls=%fused_computation.16.clone.1 | convolution fusion | flops 548929536 | bytes 13926401 | tf_op jit(solution)/shard_map/while/body/eval_jaxpr/hqk,khd->hqd/dot_general | solution.py:108
  320.2 6.1 %fusion.52 = (f32[8,512]{1,0:T(8,128)S(1)}, f32[8,512,512]{2,1,0:T(8,128)}) fusion(pred[512,512]{0,1:T(8,128)(4,1)S(1)} %compare_and_fusion.2, bf16[512,8,128]{0,2,1:T(8,128)(2,1)S(1)} %bitcast.85, bf16[512,8,128]{2,0,1:T(8,128)(2,1)} %get-tuple-element.307), kind=kOutput, calls=%fused_computation.10.clone.1 | convolution fusion | flops 543158272 | bytes 10764288 | tf_op jit(solution)/shard_map/while/body/eval_jaxpr/qhd,khd->hqk/dot_general | solution.py:100
  326.4 4.5 fusion.53
  331.4 8.5 %fusion.55 = f32[8,512,128]{2,1,0:T(8,128)} fusion(f32[8,512,128]{2,1,0:T(8,128)} %get-tuple-element.288, bf16[512,8,128]{0,2,1:T(8,128)(2,1)S(1)} %bitcast.89, f32[8,512,512]{2,1,0:T(8,128)} %get-tuple-element.268, f32[8,512]{1,0:T(8,128)S(1)} %select_maximum_fusion.2, pred[512,512]{0,1:T(8,128)(4,1)S(1)} %compare_and_fusion.2, ...), kind=kOutput, calls=%fused_computation.16.clone.1 | convolution fusion | flops 548929536 | bytes 13926401 | tf_op jit(solution)/shard_map/while/body/eval_jaxpr/hqk,khd->hqd/dot_general | solution.py:108
  345.6 6.1 %fusion.52 = (f32[8,512]{1,0:T(8,128)S(1)}, f32[8,512,512]{2,1,0:T(8,128)}) fusion(pred[512,512]{0,1:T(8,128)(4,1)S(1)} %compare_and_fusion.2, bf16[512,8,128]{0,2,1:T(8,128)(2,1)S(1)} %bitcast.85, bf16[512,8,128]{2,0,1:T(8,128)(2,1)} %get-tuple-element.307), kind=kOutput, calls=%fused_computation.10.clone.1 | convolution fusion | flops 543158272 | bytes 10764288 | tf_op jit(solution)/shard_map/while/body/eval_jaxpr/qhd,khd->hqk/dot_general | solution.py:100
  356.8 8.5 %fusion.55 = f32[8,512,128]{2,1,0:T(8,128)} fusion(f32[8,512,128]{2,1,0:T(8,128)} %get-tuple-element.288, bf16[512,8,128]{0,2,1:T(8,128)(2,1)S(1)} %bitcast.89, f32[8,512,512]{2,1,0:T(8,128)} %get-tuple-element.268, f32[8,512]{1,0:T(8,128)S(1)} %select_maximum_fusion.2, pred[512,512]{0,1:T(8,128)(4,1)S(1)} %compare_and_fusion.2, ...), kind=kOutput, calls=%fused_computation.16.clone.1 | convolution fusion | flops 548929536 | bytes 13926401 | tf_op jit(solution)/shard_map/while/body/eval_jaxpr/hqk,khd->hqd/dot_general | solution.py:108
  371.0 6.1 %fusion.52 = (f32[8,512]{1,0:T(8,128)S(1)}, f32[8,512,512]{2,1,0:T(8,128)}) fusion(pred[512,512]{0,1:T(8,128)(4,1)S(1)} %compare_and_fusion.2, bf16[512,8,128]{0,2,1:T(8,128)(2,1)S(1)} %bitcast.85, bf16[512,8,128]{2,0,1:T(8,128)(2,1)} %get-tuple-element.307), kind=kOutput, calls=%fused_computation.10.clone.1 | convolution fusion | flops 543158272 | bytes 10764288 | tf_op jit(solution)/shard_map/while/body/eval_jaxpr/qhd,khd->hqk/dot_general | solution.py:100
  382.2 8.5 %fusion.55 = f32[8,512,128]{2,1,0:T(8,128)} fusion(f32[8,512,128]{2,1,0:T(8,128)} %get-tuple-element.288, bf16[512,8,128]{0,2,1:T(8,128)(2,1)S(1)} %bitcast.89, f32[8,512,512]{2,1,0:T(8,128)} %get-tuple-element.268, f32[8,512]{1,0:T(8,128)S(1)} %select_maximum_fusion.2, pred[512,512]{0,1:T(8,128)(4,1)S(1)} %compare_and_fusion.2, ...), kind=kOutput, calls=%fused_computation.16.clone.1 | convolution fusion | flops 548929536 | bytes 13926401 | tf_op jit(solution)/shard_map/while/body/eval_jaxpr/hqk,khd->hqd/dot_general | solution.py:108
  396.4 6.1 %fusion.52 = (f32[8,512]{1,0:T(8,128)S(1)}, f32[8,512,512]{2,1,0:T(8,128)}) fusion(pred[512,512]{0,1:T(8,128)(4,1)S(1)} %compare_and_fusion.2, bf16[512,8,128]{0,2,1:T(8,128)(2,1)S(1)} %bitcast.85, bf16[512,8,128]{2,0,1:T(8,128)(2,1)} %get-tuple-element.307), kind=kOutput, calls=%fused_computation.10.clone.1 | convolution fusion | flops 543158272 | bytes 10764288 | tf_op jit(solution)/shard_map/while/body/eval_jaxpr/qhd,khd->hqk/dot_general | solution.py:100
  407.6 8.5 %fusion.55 = f32[8,512,128]{2,1,0:T(8,128)} fusion(f32[8,512,128]{2,1,0:T(8,128)} %get-tuple-element.288, bf16[512,8,128]{0,2,1:T(8,128)(2,1)S(1)} %bitcast.89, f32[8,512,512]{2,1,0:T(8,128)} %get-tuple-element.268, f32[8,512]{1,0:T(8,128)S(1)} %select_maximum_fusion.2, pred[512,512]{0,1:T(8,128)(4,1)S(1)} %compare_and_fusion.2, ...), kind=kOutput, calls=%fused_computation.16.clone.1 | convolution fusion | flops 548929536 | bytes 13926401 | tf_op jit(solution)/shard_map/while/body/eval_jaxpr/hqk,khd->hqd/dot_general | solution.py:108
  421.8 6.1 %fusion.52 = (f32[8,512]{1,0:T(8,128)S(1)}, f32[8,512,512]{2,1,0:T(8,128)}) fusion(pred[512,512]{0,1:T(8,128)(4,1)S(1)} %compare_and_fusion.2, bf16[512,8,128]{0,2,1:T(8,128)(2,1)S(1)} %bitcast.85, bf16[512,8,128]{2,0,1:T(8,128)(2,1)} %get-tuple-element.307), kind=kOutput, calls=%fused_computation.10.clone.1 | convolution fusion | flops 543158272 | bytes 10764288 | tf_op jit(solution)/shard_map/while/body/eval_jaxpr/qhd,khd->hqk/dot_general | solution.py:100
  427.9 4.5 fusion.53
  433.0 8.5 %fusion.55 = f32[8,512,128]{2,1,0:T(8,128)} fusion(f32[8,512,128]{2,1,0:T(8,128)} %get-tuple-element.288, bf16[512,8,128]{0,2,1:T(8,128)(2,1)S(1)} %bitcast.89, f32[8,512,512]{2,1,0:T(8,128)} %get-tuple-element.268, f32[8,512]{1,0:T(8,128)S(1)} %select_maximum_fusion.2, pred[512,512]{0,1:T(8,128)(4,1)S(1)} %compare_and_fusion.2, ...), kind=kOutput, calls=%fused_computation.16.clone.1 | convolution fusion | flops 548929536 | bytes 13926401 | tf_op jit(solution)/shard_map/while/body/eval_jaxpr/hqk,khd->hqd/dot_general | solution.py:108
  447.2 6.1 %fusion.52 = (f32[8,512]{1,0:T(8,128)S(1)}, f32[8,512,512]{2,1,0:T(8,128)}) fusion(pred[512,512]{0,1:T(8,128)(4,1)S(1)} %compare_and_fusion.2, bf16[512,8,128]{0,2,1:T(8,128)(2,1)S(1)} %bitcast.85, bf16[512,8,128]{2,0,1:T(8,128)(2,1)} %get-tuple-element.307), kind=kOutput, calls=%fused_computation.10.clone.1 | convolution fusion | flops 543158272 | bytes 10764288 | tf_op jit(solution)/shard_map/while/body/eval_jaxpr/qhd,khd->hqk/dot_general | solution.py:100
  453.3 4.5 fusion.53
  458.4 8.5 %fusion.55 = f32[8,512,128]{2,1,0:T(8,128)} fusion(f32[8,512,128]{2,1,0:T(8,128)} %get-tuple-element.288, bf16[512,8,128]{0,2,1:T(8,128)(2,1)S(1)} %bitcast.89, f32[8,512,512]{2,1,0:T(8,128)} %get-tuple-element.268, f32[8,512]{1,0:T(8,128)S(1)} %select_maximum_fusion.2, pred[512,512]{0,1:T(8,128)(4,1)S(1)} %compare_and_fusion.2, ...), kind=kOutput, calls=%fused_computation.16.clone.1 | convolution fusion | flops 548929536 | bytes 13926401 | tf_op jit(solution)/shard_map/while/body/eval_jaxpr/hqk,khd->hqd/dot_general | solution.py:108
  469.1 9.5 %fusion.13 = bf16[4096,512]{0,1:T(8,128)(2,1)} fusion(bf16[512,1024]{0,1:T(8,128)(2,1)S(1)} %bitcast.95, bf16[1024,4096]{1,0:T(8,128)(2,1)} %param.19), kind=kOutput, calls=%fused_computation.31 | convolution fusion | flops 4297064448 | bytes 13631488 | tf_op jit(solution)/shard_map/dot_general | solution.py:164
  492.6 23.5 %all-to-all-done.1 = bf16[8,64,1024]{2,1,0:T(8,128)(2,1)S(1)} async-done(((bf16[8,64,1024]{2,1,0:T(8,128)(2,1)}), bf16[8,64,1024]{2,1,0:T(8,128)(2,1)S(1)}, u32[]{:S(2)}, u32[]{:S(2)}) %all-to-all-start.1) | async-done | bytes 1048608 | tf_op jit(solution)/shard_map/all_to_all | solution.py:125
  523.5 6.4 %reduce-scatter.2.cloned.1.call-done = bf16[1024,512]{0,1:T(8,128)(2,1)} async-done(((bf16[4096,512]{0,1:T(8,128)(2,1)}), bf16[1024,512]{0,1:T(8,128)(2,1)}) %reduce-scatter.2.cloned.1.call-update) | async-done | bytes 1048592 | tf_op jit(solution)/shard_map/reduce_scatter | solution.py:163
  531.4 8.9 %psum.23 = f32[512]{0:T(512)S(1)} all-reduce(f32[512]{0:T(512)S(1)} %fusion.14), channel_id=1, replica_groups=mesh['tok'=8,'rep'=4] {'rep'}, use_global_device_ids=true, to_apply=%region_12.13 | all-reduce | flops 512 | bytes 4096 | tf_op jit(solution)/shard_map/psum | solution.py:174
  549.8 5.8 sort.108
  (175 shorter events, 147.2 us)
Async XLA Ops:
  7.2 5.6 copy-start.9
  7.2 2.4 copy-start
  7.2 58.0 %all-gather.4.cloned.1.call-start = ((), (), s32[]{:S(2)}) async-start(), calls=%async_computation.4 | async-start | bytes 5242880 | tf_op jit(solution)/shard_map/all_gather | solution.py:69
  7.9 173.7 %all-gather.6.cloned.1.call-start = ((), (), s32[]{:S(2)}) async-start(), calls=%async_computation.5 | async-start | bytes 9437184 | tf_op jit(solution)/shard_map/all_gather | solution.py:136
  65.2 10.6 %copy-start.8 = (bf16[512,4096]{1,0:T(8,128)(2,1)S(1)}, bf16[512,4096]{1,0:T(8,128)(2,1)}, u32[]{:S(2)}) copy-start(bf16[512,4096]{1,0:T(8,128)(2,1)} %all-gather.4.cloned.1.call-done) | copy-start | bytes 12582916
  75.8 16.0 %copy-start.5 = (f32[1024]{0:T(1024)S(1)}, f32[1024]{0:T(1024)}, u32[]{:S(2)}) copy-start(f32[1024]{0:T(1024)} %param.21) | copy-start | bytes 12292
  94.1 0.7 copy-start.6
  99.4 10.5 %copy-start.3 = (s32[4096]{0:T(1024)S(1)}, s32[4096]{0:T(1024)}, u32[]{:S(2)}) copy-start(s32[4096]{0:T(1024)} %param.25) | copy-start | bytes 49156
  99.4 164.9 %all-gather.8.cloned.1.call-start = ((), (), s32[]{:S(2)}) async-start(), calls=%async_computation.6 | async-start | bytes 9437184 | tf_op jit(solution)/shard_map/all_gather | solution.py:137
  109.8 420.1 %reduce-scatter.2.cloned.1.call-start = ((), (), s32[]{:S(2)}) async-start(), calls=%async_computation.7 | async-start | bytes 5242880 | tf_op jit(solution)/shard_map/reduce_scatter | solution.py:163
  478.6 0.7 copy-start.4
  478.6 4.6 copy-start.1
  485.9 3.9 copy-start.2
  485.9 30.2 %all-to-all-start.1 = ((bf16[8,64,1024]{2,1,0:T(8,128)(2,1)}), bf16[8,64,1024]{2,1,0:T(8,128)(2,1)S(1)}, u32[]{:S(2)}, u32[]{:S(2)}) async-start(bf16[8,64,1024]{2,1,0:T(8,128)(2,1)} %bitcast.10), calls=%async_computation.2 | async-start | bytes 2097152 | tf_op jit(solution)/shard_map/all_to_all | solution.py:125
  492.6 47.7 %copy-start.7 = (f32[1024]{0:T(1024)S(1)}, f32[1024]{0:T(1024)}, u32[]{:S(2)}) copy-start(f32[1024]{0:T(1024)} %param.22) | copy-start | bytes 12292
  516.1 30.1 %all-to-all-start.2 = ((bf16[8,64,1024]{2,1,0:T(8,128)(2,1)}), bf16[8,64,1024]{2,1,0:T(8,128)(2,1)S(1)}, u32[]{:S(2)}, u32[]{:S(2)}) async-start(bf16[8,64,1024]{2,1,0:T(8,128)(2,1)} %bitcast.12), calls=%async_computation.3 | async-start | bytes 2097152 | tf_op jit(solution)/shard_map/all_to_all | solution.py:128
  546.2 30.8 %all-to-all-start = ((bf16[8,64,1024]{2,1,0:T(8,128)(2,1)}), bf16[8,64,1024]{2,1,0:T(8,128)(2,1)S(1)}, u32[]{:S(2)}, u32[]{:S(2)}) async-start(bf16[8,64,1024]{2,1,0:T(8,128)(2,1)} %bitcast.92), calls=%async_computation.1 | async-start | bytes 2097152 | tf_op jit(solution)/shard_map/all_to_all | solution.py:180
Sparse Core Ops, SparseCore 0:
  9.8 55.2 all-gather.3
  99.5 82.0 all-gather.5
  183.8 80.5 all-gather.7
  478.7 51.1 reduce-scatter.1
where the time goes:
time: 587 us; the launch traced here: 586 us
  waiting for transfers between devices  236 us (40%)
  matrix products  153 us (26%)
  other arithmetic  80.8 us (14%)
  local copies, waits for them, and re-layouts  72.4 us (12%)
  blocking collectives  17.9 us (3%)
  between operations  14.1 us (2%)
  starting transfers between devices  11.4 us (2%)
    all_gather x1, waiting for transfers between devices, body(): lax.all_gather(value_half, 'tok', axis=0, tiled=True)  82.7 us
    all_gather x1, waiting for transfers between devices, body(): lax.all_gather(key_rot, 'tok', axis=0, tiled=True)  70.1 us
    dot_general x8, matrix products, attend(): jnp.einsum('hqk,khd->hqd', weights.astype(jnp.bfloat16), block_values, pr...  67.1 us
    all_gather x1, waiting for transfers between devices, body(): pieces = lax.all_gather(hidden_in, 'rep', axis=1, tiled=True)  51.3 us
    dot_general x8, matrix products, attend(): jnp.einsum('qhd,khd->hqk', query_rot, block_keys, preferred_element_type=...  49 us
    reduce_sum x8, other arithmetic, attend(): totals = totals * factor + jnp.sum(weights, axis=2)  35.9 us
    gather x8, local copies, waits for them, and re-layouts, attend(): key_segment = segment_ids[key_packed]  25.1 us
    all_to_all x1, waiting for transfers between devices, body(): lax.all_to_all(bucketed(key_rot, slot_order, shards), 'tok', split_axis=0...  23.5 us
  transfers between devices with their start and end apart: 7, of which 6 were waited for; matrix products, arithmetic and copies ran while one was open for 11% of the time, Pallas kernels for 0%

commit v1 on v0

--- a/solution.py
+++ b/solution.py
@@ -7,6 +7,9 @@
 HEAD_DIM = 128
 EPSILON = 1e-06
 ROPE_BASE = 500000.0
+array_link = lambda content: jnp.concatenate(
+    lax.all_to_all(jnp.stack(lax.axis_size("rep") * [content]), "rep", 0, 0), axis=1
+)
 
 
 def rotate(values, positions):
@@ -66,7 +69,7 @@
         jnp.where(my_segment[:, None] == prompt_ids[None, :], prompt_starts[None, :], 0), axis=1
     )
     positions = my_packed - my_start
-    pieces = lax.all_gather(hidden_in, "rep", axis=1, tiled=True)
+    pieces = array_link(hidden_in)
     query_rows = jnp.dot(pieces, w_query, preferred_element_type=jnp.float32)
     key_rows = jnp.dot(pieces, w_key, preferred_element_type=jnp.float32)
     value_rows = jnp.dot(pieces, w_value, preferred_element_type=jnp.float32)

time: 587 us -> 589 us (level)
  waiting for transfers between devices: 236 us -> 229 us
    all_gather x1 -> x0, waiting for transfers between devices: 51.3 us -> none  [body(): pieces = lax.all_gather(hidden_in, 'rep', axis=1, tiled=True)]
    all_to_all x0 -> x1, waiting for transfers between devices: none -> 44 us  [lax.all_to_all(jnp.stack(lax.axis_size('rep') * [content]), 'rep', 0, 0)]
where the time goes in v1:
time: 589 us; the launch traced here: 588 us
  waiting for transfers between devices  229 us (39%)
  matrix products  155 us (26%)
  other arithmetic  79.5 us (13%)
  local copies, waits for them, and re-layouts  76.1 us (13%)
  blocking collectives  18.1 us (3%)
  starting transfers between devices  16.5 us (3%)
  between operations  14 us (2%)
    all_gather x1, waiting for transfers between devices, body(): lax.all_gather(value_half, 'tok', axis=0, tiled=True)  82.7 us
    all_gather x1, waiting for transfers between devices, body(): lax.all_gather(key_rot, 'tok', axis=0, tiled=True)  70.9 us
    dot_general x8, matrix products, attend(): jnp.einsum('hqk,khd->hqd', weights.astype(jnp.bfloat16), block_values, pr...  67.1 us
    dot_general x8, matrix products, attend(): jnp.einsum('qhd,khd->hqk', query_rot, block_keys, preferred_element_type=...  49 us
    all_to_all x1, waiting for transfers between devices, lax.all_to_all(jnp.stack(lax.axis_size('rep') * [content]), 'rep', 0, 0)  44 us
    reduce_sum x8, other arithmetic, attend(): totals = totals * factor + jnp.sum(weights, axis=2)  35.9 us
    gather x8, local copies, waits for them, and re-layouts, attend(): key_segment = segment_ids[key_packed]  25.1 us
    all_to_all x1, waiting for transfers between devices, body(): lax.all_to_all(bucketed(key_rot, slot_order, shards), 'tok', split_axis=0...  23.4 us
  transfers between devices with their start and end apart: 7, of which 6 were waited for; matrix products, arithmetic and copies ran while one was open for 11% of the time, Pallas kernels for 0%

profile of v1, /device:TPU:0, one launch (start us, length us, event | category | flops | bytes accessed | tf_op | source)
XLA Modules:
  0.0 587.9 jit_solution(13691495882081726248)
XLA Ops:
  10.9 5.3 all-to-all-start
  20.8 44.0 %all-to-all-done = bf16[4,512,1024]{1,2,0:T(8,128)(2,1)} async-done(((bf16[4,512,1024]{1,2,0:T(8,128)(2,1)}), bf16[4,512,1024]{1,2,0:T(8,128)(2,1)}, u32[]{:S(2)}, u32[]{:S(2)}) %all-to-all-start) | async-done | bytes 4194336 | tf_op jit(solution)/shard_map/all_to_all | solution.py:11
  64.8 10.5 %multiply_reduce_fusion.1 = (f32[512]{0:T(512)S(1)}, f32[512,1024]{1,0:T(8,128)}) fusion(bf16[512,4096]{0,1:T(8,128)(2,1)} %bitcast.1, bf16[4096,1024]{1,0:T(8,128)(2,1)} %param.17), kind=kOutput, calls=%fused_computation.47 | convolution fusion | flops 4296015360 | bytes 14682112 | tf_op jit(solution)/shard_map/dot_general | solution.py:74
  75.4 8.4 %multiply_reduce_fusion = (f32[512]{0:T(512)S(1)}, f32[512,1024]{1,0:T(8,128)S(1)}) fusion(bf16[512,4096]{0,1:T(8,128)(2,1)} %bitcast.1, bf16[4096,1024]{1,0:T(8,128)(2,1)} %param.16), kind=kOutput, calls=%fused_computation.43 | convolution fusion | flops 4296015360 | bytes 14682112 | tf_op jit(solution)/shard_map/dot_general | solution.py:73
  83.7 9.1 %all-reduce = (f32[512]{0:T(512)S(1)}, f32[512]{0:T(512)S(1)}) all-reduce(f32[512]{0:T(512)S(1)} %get-tuple-element.181, f32[512]{0:T(512)S(1)} %get-tuple-element.183), channel_id=1, replica_groups=mesh['tok'=8,'rep'=4] {'rep'}, use_global_device_ids=true, to_apply=%region_1.2 | all-reduce | flops 1024 | bytes 8192 | tf_op jit(solution)/shard_map/psum | solution.py:76
  100.5 10.1 %convolution_convert_fusion.1 = bf16[512,1024]{1,0:T(8,128)(2,1)} fusion(bf16[512,4096]{0,1:T(8,128)(2,1)} %bitcast.1, bf16[4096,1024]{1,0:T(8,128)(2,1)} %param.18), kind=kOutput, calls=%fused_computation.48 | convolution fusion | flops 4295491584 | bytes 13631488 | tf_op jit(solution)/shard_map/dot_general | solution.py:75
  112.3 70.9 %all-gather.3.cloned.1.call-done = bf16[4096,1024]{1,0:T(8,128)(2,1)} async-done(((bf16[512,1024]{1,0:T(8,128)(2,1)}), bf16[4096,1024]{1,0:T(8,128)(2,1)}) %all-gather.3.cloned.1.call-update) | async-done | bytes 8388624 | tf_op jit(solution)/shard_map/all_gather | solution.py:139
  183.2 82.7 %all-gather.5.cloned.1.call-done = bf16[4096,1024]{1,0:T(8,128)(2,1)} async-done(((bf16[512,1024]{1,0:T(8,128)(2,1)}), bf16[4096,1024]{1,0:T(8,128)(2,1)}) %all-gather.5.cloned.1.call-update) | async-done | bytes 8388624 | tf_op jit(solution)/shard_map/all_gather | solution.py:140
  265.9 202.6 %while.15 = (s32[]{:T(128)}, f32[8,512]{1,0:T(8,128)S(1)}, f32[8,512]{1,0:T(8,128)S(1)}, f32[8,512,128]{2,1,0:T(8,128)}, s32[8,512]{1,0:T(8,128)S(1)}, /*index=5...) while((s32[]{:T(128)}, f32[8,512]{1,0:T(8,128)S(1)}, ...), condition=%wide.region_9.10_spmd.clone, body=%wide.region_6.9_spmd.clone.sunk | while | flops 1103387136 | bytes 42231948 | solution.py:149
  271.7 6.1 %fusion.52 = (f32[8,512]{1,0:T(8,128)S(1)}, f32[8,512,512]{2,1,0:T(8,128)}) fusion(pred[512,512]{0,1:T(8,128)(4,1)S(1)} %compare_and_fusion.2, bf16[512,8,128]{0,2,1:T(8,128)(2,1)S(1)} %bitcast.88, bf16[512,8,128]{2,0,1:T(8,128)(2,1)} %get-tuple-element.307), kind=kOutput, calls=%fused_computation.10.clone.1 | convolution fusion | flops 543158272 | bytes 10764288 | tf_op jit(solution)/shard_map/while/body/eval_jaxpr/qhd,khd->hqk/dot_general | solution.py:103
  277.8 4.5 fusion.53
  282.9 7.9 %fusion.55 = f32[8,512,128]{2,1,0:T(8,128)} fusion(f32[8,512,128]{2,1,0:T(8,128)} %get-tuple-element.288, bf16[512,8,128]{0,2,1:T(8,128)(2,1)S(1)} %bitcast.92, f32[8,512,512]{2,1,0:T(8,128)} %get-tuple-element.268, f32[8,512]{1,0:T(8,128)S(1)} %select_maximum_fusion.2, pred[512,512]{0,1:T(8,128)(4,1)S(1)} %compare_and_fusion.2, ...), kind=kOutput, calls=%fused_computation.16.clone.1 | convolution fusion | flops 548929536 | bytes 13926401 | tf_op jit(solution)/shard_map/while/body/eval_jaxpr/hqk,khd->hqd/dot_general | solution.py:111
  296.5 6.1 %fusion.52 = (f32[8,512]{1,0:T(8,128)S(1)}, f32[8,512,512]{2,1,0:T(8,128)}) fusion(pred[512,512]{0,1:T(8,128)(4,1)S(1)} %compare_and_fusion.2, bf16[512,8,128]{0,2,1:T(8,128)(2,1)S(1)} %bitcast.88, bf16[512,8,128]{2,0,1:T(8,128)(2,1)} %get-tuple-element.307), kind=kOutput, calls=%fused_computation.10.clone.1 | convolution fusion | flops 543158272 | bytes 10764288 | tf_op jit(solution)/shard_map/while/body/eval_jaxpr/qhd,khd->hqk/dot_general | solution.py:103
  302.6 4.5 fusion.53
  307.7 8.5 %fusion.55 = f32[8,512,128]{2,1,0:T(8,128)} fusion(f32[8,512,128]{2,1,0:T(8,128)} %get-tuple-element.288, bf16[512,8,128]{0,2,1:T(8,128)(2,1)S(1)} %bitcast.92, f32[8,512,512]{2,1,0:T(8,128)} %get-tuple-element.268, f32[8,512]{1,0:T(8,128)S(1)} %select_maximum_fusion.2, pred[512,512]{0,1:T(8,128)(4,1)S(1)} %compare_and_fusion.2, ...), kind=kOutput, calls=%fused_computation.16.clone.1 | convolution fusion | flops 548929536 | bytes 13926401 | tf_op jit(solution)/shard_map/while/body/eval_jaxpr/hqk,khd->hqd/dot_general | solution.py:111
  321.9 6.1 %fusion.52 = (f32[8,512]{1,0:T(8,128)S(1)}, f32[8,512,512]{2,1,0:T(8,128)}) fusion(pred[512,512]{0,1:T(8,128)(4,1)S(1)} %compare_and_fusion.2, bf16[512,8,128]{0,2,1:T(8,128)(2,1)S(1)} %bitcast.88, bf16[512,8,128]{2,0,1:T(8,128)(2,1)} %get-tuple-element.307), kind=kOutput, calls=%fused_computation.10.clone.1 | convolution fusion | flops 543158272 | bytes 10764288 | tf_op jit(solution)/shard_map/while/body/eval_jaxpr/qhd,khd->hqk/dot_general | solution.py:103
  333.1 8.5 %fusion.55 = f32[8,512,128]{2,1,0:T(8,128)} fusion(f32[8,512,128]{2,1,0:T(8,128)} %get-tuple-element.288, bf16[512,8,128]{0,2,1:T(8,128)(2,1)S(1)} %bitcast.92, f32[8,512,512]{2,1,0:T(8,128)} %get-tuple-element.268, f32[8,512]{1,0:T(8,128)S(1)} %select_maximum_fusion.2, pred[512,512]{0,1:T(8,128)(4,1)S(1)} %compare_and_fusion.2, ...), kind=kOutput, calls=%fused_computation.16.clone.1 | convolution fusion | flops 548929536 | bytes 13926401 | tf_op jit(solution)/shard_map/while/body/eval_jaxpr/hqk,khd->hqd/dot_general | solution.py:111
  347.3 6.1 %fusion.52 = (f32[8,512]{1,0:T(8,128)S(1)}, f32[8,512,512]{2,1,0:T(8,128)}) fusion(pred[512,512]{0,1:T(8,128)(4,1)S(1)} %compare_and_fusion.2, bf16[512,8,128]{0,2,1:T(8,128)(2,1)S(1)} %bitcast.88, bf16[512,8,128]{2,0,1:T(8,128)(2,1)} %get-tuple-element.307), kind=kOutput, calls=%fused_computation.10.clone.1 | convolution fusion | flops 543158272 | bytes 10764288 | tf_op jit(solution)/shard_map/while/body/eval_jaxpr/qhd,khd->hqk/dot_general | solution.py:103
  358.5 8.5 %fusion.55 = f32[8,512,128]{2,1,0:T(8,128)} fusion(f32[8,512,128]{2,1,0:T(8,128)} %get-tuple-element.288, bf16[512,8,128]{0,2,1:T(8,128)(2,1)S(1)} %bitcast.92, f32[8,512,512]{2,1,0:T(8,128)} %get-tuple-element.268, f32[8,512]{1,0:T(8,128)S(1)} %select_maximum_fusion.2, pred[512,512]{0,1:T(8,128)(4,1)S(1)} %compare_and_fusion.2, ...), kind=kOutput, calls=%fused_computation.16.clone.1 | convolution fusion | flops 548929536 | bytes 13926401 | tf_op jit(solution)/shard_map/while/body/eval_jaxpr/hqk,khd->hqd/dot_general | solution.py:111
  372.7 6.1 %fusion.52 = (f32[8,512]{1,0:T(8,128)S(1)}, f32[8,512,512]{2,1,0:T(8,128)}) fusion(pred[512,512]{0,1:T(8,128)(4,1)S(1)} %compare_and_fusion.2, bf16[512,8,128]{0,2,1:T(8,128)(2,1)S(1)} %bitcast.88, bf16[512,8,128]{2,0,1:T(8,128)(2,1)} %get-tuple-element.307), kind=kOutput, calls=%fused_computation.10.clone.1 | convolution fusion | flops 543158272 | bytes 10764288 | tf_op jit(solution)/shard_map/while/body/eval_jaxpr/qhd,khd->hqk/dot_general | solution.py:103
  383.8 8.5 %fusion.55 = f32[8,512,128]{2,1,0:T(8,128)} fusion(f32[8,512,128]{2,1,0:T(8,128)} %get-tuple-element.288, bf16[512,8,128]{0,2,1:T(8,128)(2,1)S(1)} %bitcast.92, f32[8,512,512]{2,1,0:T(8,128)} %get-tuple-element.268, f32[8,512]{1,0:T(8,128)S(1)} %select_maximum_fusion.2, pred[512,512]{0,1:T(8,128)(4,1)S(1)} %compare_and_fusion.2, ...), kind=kOutput, calls=%fused_computation.16.clone.1 | convolution fusion | flops 548929536 | bytes 13926401 | tf_op jit(solution)/shard_map/while/body/eval_jaxpr/hqk,khd->hqd/dot_general | solution.py:111
  398.1 6.1 %fusion.52 = (f32[8,512]{1,0:T(8,128)S(1)}, f32[8,512,512]{2,1,0:T(8,128)}) fusion(pred[512,512]{0,1:T(8,128)(4,1)S(1)} %compare_and_fusion.2, bf16[512,8,128]{0,2,1:T(8,128)(2,1)S(1)} %bitcast.88, bf16[512,8,128]{2,0,1:T(8,128)(2,1)} %get-tuple-element.307), kind=kOutput, calls=%fused_computation.10.clone.1 | convolution fusion | flops 543158272 | bytes 10764288 | tf_op jit(solution)/shard_map/while/body/eval_jaxpr/qhd,khd->hqk/dot_general | solution.py:103
  409.2 8.5 %fusion.55 = f32[8,512,128]{2,1,0:T(8,128)} fusion(f32[8,512,128]{2,1,0:T(8,128)} %get-tuple-element.288, bf16[512,8,128]{0,2,1:T(8,128)(2,1)S(1)} %bitcast.92, f32[8,512,512]{2,1,0:T(8,128)} %get-tuple-element.268, f32[8,512]{1,0:T(8,128)S(1)} %select_maximum_fusion.2, pred[512,512]{0,1:T(8,128)(4,1)S(1)} %compare_and_fusion.2, ...), kind=kOutput, calls=%fused_computation.16.clone.1 | convolution fusion | flops 548929536 | bytes 13926401 | tf_op jit(solution)/shard_map/while/body/eval_jaxpr/hqk,khd->hqd/dot_general | solution.py:111
  423.4 6.1 %fusion.52 = (f32[8,512]{1,0:T(8,128)S(1)}, f32[8,512,512]{2,1,0:T(8,128)}) fusion(pred[512,512]{0,1:T(8,128)(4,1)S(1)} %compare_and_fusion.2, bf16[512,8,128]{0,2,1:T(8,128)(2,1)S(1)} %bitcast.88, bf16[512,8,128]{2,0,1:T(8,128)(2,1)} %get-tuple-element.307), kind=kOutput, calls=%fused_computation.10.clone.1 | convolution fusion | flops 543158272 | bytes 10764288 | tf_op jit(solution)/shard_map/while/body/eval_jaxpr/qhd,khd->hqk/dot_general | solution.py:103
  434.6 8.5 %fusion.55 = f32[8,512,128]{2,1,0:T(8,128)} fusion(f32[8,512,128]{2,1,0:T(8,128)} %get-tuple-element.288, bf16[512,8,128]{0,2,1:T(8,128)(2,1)S(1)} %bitcast.92, f32[8,512,512]{2,1,0:T(8,128)} %get-tuple-element.268, f32[8,512]{1,0:T(8,128)S(1)} %select_maximum_fusion.2, pred[512,512]{0,1:T(8,128)(4,1)S(1)} %compare_and_fusion.2, ...), kind=kOutput, calls=%fused_computation.16.clone.1 | convolution fusion | flops 548929536 | bytes 13926401 | tf_op jit(solution)/shard_map/while/body/eval_jaxpr/hqk,khd->hqd/dot_general | solution.py:111
  448.8 6.1 %fusion.52 = (f32[8,512]{1,0:T(8,128)S(1)}, f32[8,512,512]{2,1,0:T(8,128)}) fusion(pred[512,512]{0,1:T(8,128)(4,1)S(1)} %compare_and_fusion.2, bf16[512,8,128]{0,2,1:T(8,128)(2,1)S(1)} %bitcast.88, bf16[512,8,128]{2,0,1:T(8,128)(2,1)} %get-tuple-element.307), kind=kOutput, calls=%fused_computation.10.clone.1 | convolution fusion | flops 543158272 | bytes 10764288 | tf_op jit(solution)/shard_map/while/body/eval_jaxpr/qhd,khd->hqk/dot_general | solution.py:103
  460.0 8.5 %fusion.55 = f32[8,512,128]{2,1,0:T(8,128)} fusion(f32[8,512,128]{2,1,0:T(8,128)} %get-tuple-element.288, bf16[512,8,128]{0,2,1:T(8,128)(2,1)S(1)} %bitcast.92, f32[8,512,512]{2,1,0:T(8,128)} %get-tuple-element.268, f32[8,512]{1,0:T(8,128)S(1)} %select_maximum_fusion.2, pred[512,512]{0,1:T(8,128)(4,1)S(1)} %compare_and_fusion.2, ...), kind=kOutput, calls=%fused_computation.16.clone.1 | convolution fusion | flops 548929536 | bytes 13926401 | tf_op jit(solution)/shard_map/while/body/eval_jaxpr/hqk,khd->hqd/dot_general | solution.py:111
  470.7 9.5 %fusion.13 = bf16[4096,512]{0,1:T(8,128)(2,1)} fusion(bf16[512,1024]{0,1:T(8,128)(2,1)S(1)} %bitcast.98, bf16[1024,4096]{1,0:T(8,128)(2,1)} %param.19), kind=kOutput, calls=%fused_computation.31 | convolution fusion | flops 4297064448 | bytes 13631488 | tf_op jit(solution)/shard_map/dot_general | solution.py:167
  494.3 23.4 %all-to-all-done.2 = bf16[8,64,1024]{2,1,0:T(8,128)(2,1)S(1)} async-done(((bf16[8,64,1024]{2,1,0:T(8,128)(2,1)}), bf16[8,64,1024]{2,1,0:T(8,128)(2,1)S(1)}, u32[]{:S(2)}, u32[]{:S(2)}) %all-to-all-start.2) | async-done | bytes 1048608 | tf_op jit(solution)/shard_map/all_to_all | solution.py:128
  525.1 6.4 %reduce-scatter.2.cloned.1.call-done = bf16[1024,512]{0,1:T(8,128)(2,1)} async-done(((bf16[4096,512]{0,1:T(8,128)(2,1)}), bf16[1024,512]{0,1:T(8,128)(2,1)}) %reduce-scatter.2.cloned.1.call-update) | async-done | bytes 1048592 | tf_op jit(solution)/shard_map/reduce_scatter | solution.py:166
  533.0 8.9 %psum.23 = f32[512]{0:T(512)S(1)} all-reduce(f32[512]{0:T(512)S(1)} %fusion.14), channel_id=1, replica_groups=mesh['tok'=8,'rep'=4] {'rep'}, use_global_device_ids=true, to_apply=%region_12.13 | all-reduce | flops 512 | bytes 4096 | tf_op jit(solution)/shard_map/psum | solution.py:177
  551.4 5.8 sort.108
  (174 shorter events, 153.2 us)
Async XLA Ops:
  10.9 5.3 copy-start.8
  10.9 5.5 copy-start.3
  10.9 5.6 copy-start
  10.9 53.9 %all-to-all-start = ((bf16[4,512,1024]{1,2,0:T(8,128)(2,1)}), bf16[4,512,1024]{1,2,0:T(8,128)(2,1)}, u32[]{:S(2)}, u32[]{:S(2)}) async-start(bf16[4,512,1024]{1,2,0:T(8,128)(2,1)} %stack.2), calls=%async_computation | async-start | bytes 8388608 | tf_op jit(solution)/shard_map/all_to_all | solution.py:11
  16.3 166.9 %all-gather.3.cloned.1.call-start = ((), (), s32[]{:S(2)}) async-start(), calls=%async_computation.5 | async-start | bytes 9437184 | tf_op jit(solution)/shard_map/all_gather | solution.py:139
  75.4 17.5 %copy-start.5 = (f32[1024]{0:T(1024)S(1)}, f32[1024]{0:T(1024)}, u32[]{:S(2)}) copy-start(f32[1024]{0:T(1024)} %param.21) | copy-start | bytes 12292
  95.2 0.7 copy-start.6
  100.5 165.4 %all-gather.5.cloned.1.call-start = ((), (), s32[]{:S(2)}) async-start(), calls=%async_computation.6 | async-start | bytes 9437184 | tf_op jit(solution)/shard_map/all_gather | solution.py:140
  110.7 420.8 %reduce-scatter.2.cloned.1.call-start = ((), (), s32[]{:S(2)}) async-start(), calls=%async_computation.7 | async-start | bytes 5242880 | tf_op jit(solution)/shard_map/reduce_scatter | solution.py:166
  480.2 0.7 copy-start.4
  480.2 4.6 copy-start.1
  487.6 4.0 copy-start.2
  487.6 30.2 %all-to-all-start.2 = ((bf16[8,64,1024]{2,1,0:T(8,128)(2,1)}), bf16[8,64,1024]{2,1,0:T(8,128)(2,1)S(1)}, u32[]{:S(2)}, u32[]{:S(2)}) async-start(bf16[8,64,1024]{2,1,0:T(8,128)(2,1)} %bitcast.13), calls=%async_computation.3 | async-start | bytes 2097152 | tf_op jit(solution)/shard_map/all_to_all | solution.py:128
  494.3 47.6 %copy-start.7 = (f32[1024]{0:T(1024)S(1)}, f32[1024]{0:T(1024)}, u32[]{:S(2)}) copy-start(f32[1024]{0:T(1024)} %param.22) | copy-start | bytes 12292
  517.8 30.1 %all-to-all-start.3 = ((bf16[8,64,1024]{2,1,0:T(8,128)(2,1)}), bf16[8,64,1024]{2,1,0:T(8,128)(2,1)S(1)}, u32[]{:S(2)}, u32[]{:S(2)}) async-start(bf16[8,64,1024]{2,1,0:T(8,128)(2,1)} %bitcast.15), calls=%async_computation.4 | async-start | bytes 2097152 | tf_op jit(solution)/shard_map/all_to_all | solution.py:131
  547.8 30.8 %all-to-all-start.1 = ((bf16[8,64,1024]{2,1,0:T(8,128)(2,1)}), bf16[8,64,1024]{2,1,0:T(8,128)(2,1)S(1)}, u32[]{:S(2)}, u32[]{:S(2)}) async-start(bf16[8,64,1024]{2,1,0:T(8,128)(2,1)} %bitcast.95), calls=%async_computation.2 | async-start | bytes 2097152 | tf_op jit(solution)/shard_map/all_to_all | solution.py:183
Sparse Core Ops, SparseCore 0:
  100.6 82.5 all-gather.2
  185.4 80.5 all-gather.4
  480.4 51.1 reduce-scatter.1
